TPU v7x, 512 devices: a whole 4x4x16 slice. The times are simulated.
512 devices in a mesh: dp: 32 (over z, y_hi), seq: 16 (over y_lo, x, core).
Axes of the slice: x: 4, y: 4 (y_hi: 2, y_lo: 2; y = y_hi * 2 + y_lo), z: 16, core: 2. Of those that a mesh axis runs over, the one named last changes fastest.
Arguments:
- sequence_in: bfloat16 [32, 8192, 768], P('dp', 'seq'), may hold values from -6 to 6
- output_grad: bfloat16 [32, 8192, 768], P('dp', 'seq'), may hold values from -6 to 6
- skip_mask: int32 [32, 2], P('dp'), may hold values 0 or 1
- in_gain: float32 [2, 768], replicated, may hold values from 0.25 to 1.75
- input_shift_vec: float32 [2, 768], replicated, may hold values from -3 to 3
- mid_gain: float32 [2, 384], replicated, may hold values from 0.25 to 1.75
- mid_offset: float32 [2, 384], replicated, may hold values from -3 to 3
- conv_weight: bfloat16 [2, 3, 768, 384], P(None, None, 'seq'), may hold values from -0.21875 to 0.21875
- point_weight: bfloat16 [384, 2, 768], P('seq'), may hold values from -0.3125 to 0.3125
Outputs:
- point_grad: float32 [384, 2, 768], P('seq')
- input_grad: bfloat16 [32, 8192, 768], P('dp', 'seq')
Inputs may be any that keep to these rules, and one draw needn't show every extreme that they name: skip_mask[s, b] = 1 means that sample s passes block b unchanged in this step.
All inputs are finite; a program needn't handle non-finite values.
Results may differ from a plain program's by a relative error of at most 0.009.
Values may be sent and summed in bfloat16 or wider, within the bound.
No kernel may reach another device: no remote copies, remote signals or barrier semaphores. Data moves between devices by JAX's collectives and lax.ppermute only.
A program may use at most 64 MiB of HBM per device.

v0:
```python
import math
import jax
import jax.numpy as jnp
from jax import lax
from jax.sharding import PartitionSpec as P

FIRST_DILATION = 1024
SECOND_DILATION = 2048


def passed_along(value, axis, by):
    peers = lax.axis_size(axis)
    pairs = [(i, i + by) for i in range(peers) if 0 <= i + by < peers]
    return lax.ppermute(value, axis, pairs)


def gelu_tanh(values):
    return jax.nn.gelu(values, approximate=True)


def contract_last(left, right):
    return lax.dot_general(
        left, right, (((1,), (1,)), ((), ())), preferred_element_type=jnp.float32
    )


def neighbours(source, shards_away):
    earlier = passed_along(source, "seq", shards_away)
    later = passed_along(source, "seq", -shards_away)
    return (earlier, later)


def forward_local(
    state, earlier, activated, later, weight, gain_vec, offset_vec, projection, kept_flag
):
    conv_out = jnp.dot(earlier, weight[0], preferred_element_type=jnp.float32)
    conv_out = conv_out + jnp.dot(activated, weight[1], preferred_element_type=jnp.float32)
    conv_out = conv_out + jnp.dot(later, weight[2], preferred_element_type=jnp.float32)
    middle = conv_out * gain_vec + offset_vec
    hidden_act = gelu_tanh(middle).astype(jnp.bfloat16)
    branch = jnp.dot(hidden_act, projection, preferred_element_type=jnp.float32)
    result = (state.astype(jnp.float32) + kept_flag * branch).astype(jnp.bfloat16)
    return (middle, hidden_act, result)


def backward_first(gradient, middle, projection, gain_vec, kept_flag):
    branch_grad = (kept_flag * gradient.astype(jnp.float32)).astype(jnp.bfloat16)
    hidden_grad = contract_last(branch_grad, projection)
    middle_grad = jax.vjp(gelu_tanh, middle)[1](hidden_grad)[0]
    conv_grad = (middle_grad * gain_vec).astype(jnp.bfloat16)
    return (conv_grad, branch_grad)


def backward_second(gradient, earlier, conv_grad, later, weight, normed, gain_vec):
    act_grad = (
        contract_last(later, weight[0])
        + contract_last(conv_grad, weight[1])
        + contract_last(earlier, weight[2])
    )
    normed_grad = jax.vjp(gelu_tanh, normed)[1](act_grad)[0] * gain_vec
    return (gradient.astype(jnp.float32) + normed_grad).astype(jnp.bfloat16)


def grad_rows(hidden_act, branch_grad):
    return lax.dot_general(
        hidden_act, branch_grad, (((0,), (0,)), ((), ())), preferred_element_type=jnp.float32
    )


def shards(
    sequence_in,
    output_grad,
    skip_mask,
    in_gain,
    input_shift_vec,
    mid_gain,
    mid_offset,
    conv_weight,
    point_weight,
):
    position_list = sequence_in.shape[1]
    channels = sequence_in.shape[2]
    point_full = lax.all_gather(point_weight, "seq", axis=0, tiled=True)
    neighbour_reach = (FIRST_DILATION // position_list, SECOND_DILATION // position_list)
    state = sequence_in.reshape(-1, channels)
    total_rows = state.shape[0]
    saved = []
    kept_weights = []
    for block_index in range(2):
        kept_flag = (1 - skip_mask[0, block_index]).astype(jnp.float32)
        normed = state.astype(jnp.float32) * in_gain[block_index] + input_shift_vec[block_index]
        activated = gelu_tanh(normed).astype(jnp.bfloat16)
        earlier, later = neighbours(
            activated.reshape(sequence_in.shape), neighbour_reach[block_index]
        )
        earlier = earlier.reshape(total_rows, channels)
        later = later.reshape(total_rows, channels)
        weight = lax.all_gather(conv_weight[block_index], "seq", axis=1, tiled=True)
        kept_weights.append(weight)
        operands = (
            state,
            earlier,
            activated,
            later,
            weight,
            mid_gain[block_index],
            mid_offset[block_index],
            point_full[:, block_index, :],
            kept_flag,
        )
        middle, hidden_act, state = forward_local(*operands)
        saved.append((normed, middle, hidden_act, kept_flag))
    gradient = output_grad.reshape(-1, channels)
    hidden_saved = [None, None]
    branch_saved = [None, None]
    for block_index in (1, 0):
        normed, middle, hidden_act, kept_flag = saved[block_index]
        projection = point_full[:, block_index, :]
        first_operands = (gradient, middle, projection, mid_gain[block_index], kept_flag)
        conv_grad, branch_grad = backward_first(*first_operands)
        hidden_saved[block_index] = hidden_act
        branch_saved[block_index] = branch_grad
        earlier, later = neighbours(
            conv_grad.reshape(sequence_in.shape[0], position_list, -1), neighbour_reach[block_index]
        )
        earlier = earlier.reshape(total_rows, -1)
        later = later.reshape(total_rows, -1)
        weight = lax.all_gather(conv_weight[block_index], "seq", axis=1, tiled=True)
        second_operands = (
            gradient,
            earlier,
            conv_grad,
            later,
            weight,
            normed,
            in_gain[block_index],
        )
        gradient = backward_second(*second_operands)
    first_term = grad_rows(hidden_saved[0], branch_saved[0])
    second_term = grad_rows(hidden_saved[1], branch_saved[1])
    shared_part = lax.psum_scatter(
        jnp.stack([first_term, second_term], axis=1), "seq", scatter_dimension=0, tiled=True
    )
    summed = lax.psum(shared_part, "dp")
    sample_count = sequence_in.shape[0] * lax.axis_size("dp")
    full_length = position_list * lax.axis_size("seq")
    point_grad = summed * (1.0 / math.sqrt(sample_count * full_length))
    return (point_grad, gradient.reshape(sequence_in.shape))


def solution(mesh):
    return jax.shard_map(
        shards,
        mesh=mesh,
        in_specs=(
            P("dp", "seq", None),
            P("dp", "seq", None),
            P("dp", None),
            P(),
            P(),
            P(),
            P(),
            P(None, None, "seq", None),
            P("seq", None, None),
        ),
        out_specs=(P("seq", None, None), P("dp", "seq", None)),
        check_vma=False,
    )
```

profile of v0, /device:TPU:2, one launch (start us, length us, event | category | flops | bytes accessed | tf_op | source)
XLA Modules:
  0.0 578.6 jit_solution(11100754376341167043)
XLA Ops:
  7.2 1.7 fusion.103
  9.0 1.5 copy.12
  12.1 1.8 fusion.15
  13.9 7.8 %collective-permute-start.1 = (bf16[1,512,768]{2,1,0:T(8,128)(2,1)S(1)}, bf16[1,512,768]{2,1,0:T(8,128)(2,1)S(1)}, u32[]{:S(2)}, u32[]{:S(2)}) collective-permute-start(bf16[1,512,768]{2,1,0:T(8,128)(2,1)S(1)} %fusion.15), channel_id=1, source_target_pairs={{2,0},{3,1},{4,2},{5,3},{6,4},{7,5},{8,6},{9,7},{10,8},{11,9},{12,... | collective-permute-start | bytes 2359304 | tf_op jit(solution)/shard_map/ppermute | solution.py:14
  21.7 1.9 collective-permute-start
  25.0 37.8 %all-gather.8.cloned.1.call-done = bf16[1,3,768,384]{3,2,1,0:T(8,128)(2,1)} async-done(((bf16[1,3,48,384]{3,2,1,0:T(8,128)(2,1)}), bf16[1,3,768,384]{3,2,1,0:T(8,128)(2,1)}) %all-gather.8.cloned.1.call-update) | async-done | bytes 1769488 | tf_op jit(solution)/shard_map/all_gather | solution.py:98
  62.7 1.8 fusion.70
  65.1 2.7 fusion.44
  67.8 40.6 %all-gather.6.cloned.1.call-done = bf16[384,2,768]{2,0,1:T(8,128)(2,1)} async-done(((bf16[24,2,768]{2,0,1:T(8,128)(2,1)}), bf16[384,2,768]{2,0,1:T(8,128)(2,1)}) %all-gather.6.cloned.1.call-update) | async-done | bytes 1179664 | tf_op jit(solution)/shard_map/all_gather | solution.py:83
  108.3 2.0 fusion.4
  111.0 1.3 collective-permute-start.3
  112.3 7.0 %collective-permute-start.2 = (bf16[1,512,768]{2,1,0:T(8,128)(2,1)S(1)}, bf16[1,512,768]{2,1,0:T(8,128)(2,1)}, u32[]{:S(2)}, u32[]{:S(2)}) collective-permute-start(bf16[1,512,768]{2,1,0:T(8,128)(2,1)S(1)} %fusion.102), channel_id=1, source_target_pairs={{0,4},{1,5},{2,6},{3,7},{4,8},{5,9},{6,10},{7,11},{8,12},{9,13},{1... | collective-permute-start | bytes 2359304 | tf_op jit(solution)/shard_map/ppermute | solution.py:14
  119.8 41.1 %all-gather.10.cloned.1.call-done = bf16[1,3,768,384]{3,2,1,0:T(8,128)(2,1)} async-done(((bf16[1,3,48,384]{3,2,1,0:T(8,128)(2,1)}), bf16[1,3,768,384]{3,2,1,0:T(8,128)(2,1)}) %all-gather.10.cloned.1.call-update) | async-done | bytes 1769488 | tf_op jit(solution)/shard_map/all_gather | solution.py:98
  160.9 2.0 fusion.88
  162.9 1.7 fusion.65
  164.7 1.9 fusion.41
  166.6 0.9 fusion.60
  167.5 1.3 collective-permute-start.4
  168.8 6.1 %collective-permute-start.5 = (bf16[1,512,384]{2,1,0:T(8,128)(2,1)S(1)}, bf16[1,512,384]{2,1,0:T(8,128)(2,1)S(1)}, u32[]{:S(2)}, u32[]{:S(2)}) collective-permute-start(bf16[1,512,384]{2,1,0:T(8,128)(2,1)S(1)} %bitcast.137), channel_id=1, source_target_pairs={{0,4},{1,5},{2,6},{3,7},{4,8},{5,9},{6,10},{7,11},{8,12},{9,13},{1... | collective-permute-start | bytes 1179656 | tf_op jit(solution)/shard_map/ppermute | solution.py:14
  176.2 6.6 %collective-permute-done.4 = bf16[1,512,384]{2,1,0:T(8,128)(2,1)S(1)} collective-permute-done((bf16[1,512,384]{2,1,0:T(8,128)(2,1)S(1)}, bf16[1,512,384]{2,1,0:T(8,128)(2,1)S(1)}, u32[]{:S(2)}, u32[]{:S(2)}) %collective-permute-start.4) | collective-permute-done | bytes 393248 | tf_op jit(solution)/shard_map/ppermute | solution.py:14
  183.5 1.6 fusion.22
  186.0 1.6 pad_maximum_fusion
  187.7 1.1 copy-done.10
  188.7 2.8 fusion.52
  191.5 1.9 collective-permute-start.6
  193.4 4.6 collective-permute-start.7
  198.0 1.6 fusion.84
  199.6 5.2 collective-permute-done.6
  204.8 1.7 fusion.83
  206.5 55.3 %reduce-scatter.2.cloned.1.call-done = f32[24,2,768]{2,0,1:T(8,128)} async-done(((f32[384,2,768]{2,0,1:T(8,128)}), f32[24,2,768]{2,0,1:T(8,128)}) %reduce-scatter.2.cloned.1.call-update) | async-done | bytes 147472 | tf_op jit(solution)/shard_map/reduce_scatter | solution.py:141
  261.9 4.5 fusion.77
  266.4 304.0 %all-reduce.2.cloned.1.call-done = f32[24,2,768]{2,0,1:T(8,128)} async-done(((f32[24,2,768]{2,0,1:T(8,128)}), f32[24,2,768]{2,0,1:T(8,128)}) %all-reduce.2.cloned.1.call-update) | async-done | bytes 147472 | tf_op jit(solution)/shard_map/psum | solution.py:144
  (48 shorter events, 8.1 us)
Async XLA Ops:
  7.2 16.5 %copy-start.6 = (s32[1,2]{1,0:T(1,128)S(1)}, s32[1,2]{1,0:T(1,128)}, u32[]{:S(2)}) copy-start(s32[1,2]{1,0:T(1,128)} %param.11) | copy-start | bytes 28
  7.2 17.7 %copy-start.5 = (f32[2,384]{1,0:T(2,128)S(1)}, f32[2,384]{1,0:T(2,128)}, u32[]{:S(2)}) copy-start(f32[2,384]{1,0:T(2,128)} %param.14) | copy-start | bytes 9220
  7.2 17.7 %copy-start.4 = (f32[2,384]{1,0:T(2,128)S(1)}, f32[2,384]{1,0:T(2,128)}, u32[]{:S(2)}) copy-start(f32[2,384]{1,0:T(2,128)} %param.15) | copy-start | bytes 9220
  7.2 55.5 %all-gather.8.cloned.1.call-start = ((), (), s32[]{:S(2)}) async-start(), calls=%async_computation.4 | async-start | bytes 1880064 | tf_op jit(solution)/shard_map/all_gather | solution.py:98
  8.9 99.4 %all-gather.6.cloned.1.call-start = ((), (), s32[]{:S(2)}) async-start(), calls=%async_computation.1 | async-start | bytes 1253376 | tf_op jit(solution)/shard_map/all_gather | solution.py:83
  10.5 150.4 %all-gather.10.cloned.1.call-start = ((), (), s32[]{:S(2)}) async-start(), calls=%async_computation.5 | async-start | bytes 1880064 | tf_op jit(solution)/shard_map/all_gather | solution.py:98
  11.3 250.6 %reduce-scatter.2.cloned.1.call-start = ((), (), s32[]{:S(2)}) async-start(), calls=%async_computation.2 | async-start | bytes 2506752 | tf_op jit(solution)/shard_map/reduce_scatter | solution.py:141
  13.9 50.6 %collective-permute-start.1 = (bf16[1,512,768]{2,1,0:T(8,128)(2,1)S(1)}, bf16[1,512,768]{2,1,0:T(8,128)(2,1)S(1)}, u32[]{:S(2)}, u32[]{:S(2)}) collective-permute-start(bf16[1,512,768]{2,1,0:T(8,128)(2,1)S(1)} %fusion.15), channel_id=1, source_target_pairs={{2,0},{3,1},{4,2},{5,3},{6,4},{7,5},{8,6},{9,7},{10,8},{11,9},{12,... | collective-permute-start | bytes 2359304 | tf_op jit(solution)/shard_map/ppermute | solution.py:14
  21.7 43.3 %collective-permute-start = (bf16[1,512,768]{2,1,0:T(8,128)(2,1)S(1)}, bf16[1,512,768]{2,1,0:T(8,128)(2,1)}, u32[]{:S(2)}, u32[]{:S(2)}) collective-permute-start(bf16[1,512,768]{2,1,0:T(8,128)(2,1)S(1)} %fusion.15), channel_id=1, source_target_pairs={{0,2},{1,3},{2,4},{3,5},{4,6},{5,7},{6,8},{7,9},{8,10},{9,11},{10,... | collective-permute-start | bytes 2359304 | tf_op jit(solution)/shard_map/ppermute | solution.py:14
  62.7 1.8 copy-start
  65.1 43.3 %copy-start.2 = (bf16[1,512,768]{2,1,0:T(8,128)(2,1)S(1)}, bf16[1,512,768]{2,1,0:T(8,128)(2,1)}, u32[]{:S(2)}) copy-start(bf16[1,512,768]{2,1,0:T(8,128)(2,1)} %param.9) | copy-start | bytes 2359300
  111.0 51.9 %collective-permute-start.3 = (bf16[1,512,768]{2,1,0:T(8,128)(2,1)S(1)}, bf16[1,512,768]{2,1,0:T(8,128)(2,1)}, u32[]{:S(2)}, u32[]{:S(2)}) collective-permute-start(bf16[1,512,768]{2,1,0:T(8,128)(2,1)S(1)} %fusion.102), channel_id=1, source_target_pairs={{4,0},{5,1},{6,2},{7,3},{8,4},{9,5},{10,6},{11,7},{12,8},{13,9},{1... | collective-permute-start | bytes 2359304 | tf_op jit(solution)/shard_map/ppermute | solution.py:14
  112.3 52.4 %collective-permute-start.2 = (bf16[1,512,768]{2,1,0:T(8,128)(2,1)S(1)}, bf16[1,512,768]{2,1,0:T(8,128)(2,1)}, u32[]{:S(2)}, u32[]{:S(2)}) collective-permute-start(bf16[1,512,768]{2,1,0:T(8,128)(2,1)S(1)} %fusion.102), channel_id=1, source_target_pairs={{0,4},{1,5},{2,6},{3,7},{4,8},{5,9},{6,10},{7,11},{8,12},{9,13},{1... | collective-permute-start | bytes 2359304 | tf_op jit(solution)/shard_map/ppermute | solution.py:14
  160.9 2.0 copy-start.1
  164.7 1.9 copy-start.7
  164.7 1.9 copy-start.8
  167.5 15.3 %collective-permute-start.4 = (bf16[1,512,384]{2,1,0:T(8,128)(2,1)S(1)}, bf16[1,512,384]{2,1,0:T(8,128)(2,1)S(1)}, u32[]{:S(2)}, u32[]{:S(2)}) collective-permute-start(bf16[1,512,384]{2,1,0:T(8,128)(2,1)S(1)} %bitcast.136), channel_id=1, source_target_pairs={{4,0},{5,1},{6,2},{7,3},{8,4},{9,5},{10,6},{11,7},{12,8},{13,9},{1... | collective-permute-start | bytes 1179656 | tf_op jit(solution)/shard_map/ppermute | solution.py:14
  168.8 14.7 %collective-permute-start.5 = (bf16[1,512,384]{2,1,0:T(8,128)(2,1)S(1)}, bf16[1,512,384]{2,1,0:T(8,128)(2,1)S(1)}, u32[]{:S(2)}, u32[]{:S(2)}) collective-permute-start(bf16[1,512,384]{2,1,0:T(8,128)(2,1)S(1)} %bitcast.137), channel_id=1, source_target_pairs={{0,4},{1,5},{2,6},{3,7},{4,8},{5,9},{6,10},{7,11},{8,12},{9,13},{1... | collective-permute-start | bytes 1179656 | tf_op jit(solution)/shard_map/ppermute | solution.py:14
  183.4 1.7 copy-start.3
  185.1 0.9 copy-start.9
  187.6 1.1 copy-start.10
  187.6 382.8 %all-reduce.2.cloned.1.call-start = ((), (), s32[]{:S(2)}) async-start(), calls=%async_computation.3 | async-start | bytes 294912 | tf_op jit(solution)/shard_map/psum | solution.py:144
  191.5 13.3 %collective-permute-start.6 = (bf16[1,512,384]{2,1,0:T(8,128)(2,1)}, bf16[1,512,384]{2,1,0:T(8,128)(2,1)S(1)}, u32[]{:S(2)}, u32[]{:S(2)}) collective-permute-start(bf16[1,512,384]{2,1,0:T(8,128)(2,1)} %bitcast.24), channel_id=1, source_target_pairs={{2,0},{3,1},{4,2},{5,3},{6,4},{7,5},{8,6},{9,7},{10,8},{11,9},{12,... | collective-permute-start | bytes 1179656 | tf_op jit(solution)/shard_map/ppermute | solution.py:14
  193.4 68.5 %collective-permute-start.7 = (bf16[1,512,384]{2,1,0:T(8,128)(2,1)}, bf16[1,512,384]{2,1,0:T(8,128)(2,1)}, u32[]{:S(2)}, u32[]{:S(2)}) collective-permute-start(bf16[1,512,384]{2,1,0:T(8,128)(2,1)} %bitcast.24), channel_id=1, source_target_pairs={{0,2},{1,3},{2,4},{3,5},{4,6},{5,7},{6,8},{7,9},{8,10},{9,11},{10,... | collective-permute-start | bytes 1179656 | tf_op jit(solution)/shard_map/ppermute | solution.py:14
Sparse Core Ops, SparseCore 0:
  10.7 51.9 all-gather.7
  64.8 43.4 all-gather.5
  111.0 49.8 all-gather.9
  187.7 74.0 reduce-scatter.1
  264.6 305.7 all-reduce.1
where the time goes:
time: 579 us
  waiting for transfers between devices  491 us (85%)
  starting transfers between devices  32 us (6%)
  matrix products  28.3 us (5%)
  between operations  15.3 us (3%)
  local copies, waits for them, and re-layouts  6.63 us (1%)
    psum x1, waiting for transfers between devices, shards(): summed = lax.psum(shared_part, 'dp')  304 us
    all_gather x2, waiting for transfers between devices, shards(): weight = lax.all_gather(conv_weight[block_index], 'seq', axis=1, tiled=True)  78.8 us
    reduce_scatter x1, waiting for transfers between devices, shards(): lax.psum_scatter(jnp.stack([first_term, second_term], axis=1), 'seq', sca...  55.3 us
    all_gather x1, waiting for transfers between devices, shards(): point_full = lax.all_gather(point_weight, 'seq', axis=0, tiled=True)  40.6 us
    ppermute x8, starting transfers between devices, passed_along(): return lax.ppermute(value, axis, pairs)  31.8 us
    dot_general x8, matrix products, contract_last(): lax.dot_general(left, right, (((1,), (1,)), ((), ())), preferred_element_...  14.3 us
    ppermute x8, waiting for transfers between devices, passed_along(): return lax.ppermute(value, axis, pairs)  11.9 us
  transfers between devices with their start and end apart: 13, of which 7 were waited for; matrix products, arithmetic and copies ran while one was open for 5% of the time, Pallas kernels for 0%

commit v1 on v0

--- a/solution.py
+++ b/solution.py
@@ -6,6 +6,11 @@
 
 FIRST_DILATION = 1024
 SECOND_DILATION = 2048
+
+
+def gather_and_add(x, axis):
+    blocks = lax.all_gather(x, axis)
+    return jnp.sum(blocks, axis=0)
 
 
 def passed_along(value, axis, by):
@@ -141,7 +146,7 @@
     shared_part = lax.psum_scatter(
         jnp.stack([first_term, second_term], axis=1), "seq", scatter_dimension=0, tiled=True
     )
-    summed = lax.psum(shared_part, "dp")
+    summed = gather_and_add(shared_part, "dp")
     sample_count = sequence_in.shape[0] * lax.axis_size("dp")
     full_length = position_list * lax.axis_size("seq")
     point_grad = summed * (1.0 / math.sqrt(sample_count * full_length))

time: 579 us -> 447 us (0.77)
  waiting for transfers between devices: 491 us -> 360 us
    psum x1 -> x0, waiting for transfers between devices: 304 us -> none  [shards(): summed = lax.psum(shared_part, 'dp')]
    all_gather x0 -> x1, waiting for transfers between devices: none -> 153 us  [gather_and_add(): blocks = lax.all_gather(x, axis)]
    reduce_scatter x1, waiting for transfers between devices: 55.3 us -> 74.1 us  [shards(): lax.psum_scatter(jnp.stack([first_term, second_term], axis=1), 'seq', sca...]
  transfers between devices with their start and end apart: 13 -> 13, of which waited for: 7 -> 8; matrix products, arithmetic and copies ran while one was open for 5% -> 6% of each run, Pallas kernels for 0% -> 0%
where the time goes in v1:
time: 447 us
  waiting for transfers between devices  360 us (81%)
  starting transfers between devices  34.1 us (8%)
  matrix products  23.7 us (5%)
  between operations  15.4 us (3%)
  other arithmetic  7.44 us (2%)
  local copies, waits for them, and re-layouts  5.66 us (1%)
    all_gather x1, waiting for transfers between devices, gather_and_add(): blocks = lax.all_gather(x, axis)  153 us
    all_gather x2, waiting for transfers between devices, shards(): weight = lax.all_gather(conv_weight[block_index], 'seq', axis=1, tiled=True)  79 us
    reduce_scatter x1, waiting for transfers between devices, shards(): lax.psum_scatter(jnp.stack([first_term, second_term], axis=1), 'seq', sca...  74.1 us
    all_gather x1, waiting for transfers between devices, shards(): point_full = lax.all_gather(point_weight, 'seq', axis=0, tiled=True)  40.6 us
    ppermute x8, starting transfers between devices, passed_along(): return lax.ppermute(value, axis, pairs)  33.9 us
    ppermute x8, waiting for transfers between devices, passed_along(): return lax.ppermute(value, axis, pairs)  13.2 us
    dot_general x8, matrix products, contract_last(): lax.dot_general(left, right, (((1,), (1,)), ((), ())), preferred_element_...  9.74 us
  transfers between devices with their start and end apart: 13, of which 8 were waited for; matrix products, arithmetic and copies ran while one was open for 6% of the time, Pallas kernels for 0%

profile of v1, /device:TPU:2, one launch (start us, length us, event | category | flops | bytes accessed | tf_op | source)
XLA Modules:
  0.0 446.5 jit_solution(15876528556339746028)
XLA Ops:
  7.2 1.7 fusion.103
  9.0 1.5 copy.12
  12.1 1.8 fusion.15
  13.9 7.8 %collective-permute-start.1 = (bf16[1,512,768]{2,1,0:T(8,128)(2,1)S(1)}, bf16[1,512,768]{2,1,0:T(8,128)(2,1)S(1)}, u32[]{:S(2)}, u32[]{:S(2)}) collective-permute-start(bf16[1,512,768]{2,1,0:T(8,128)(2,1)S(1)} %fusion.15), channel_id=1, source_target_pairs={{2,0},{3,1},{4,2},{5,3},{6,4},{7,5},{8,6},{9,7},{10,8},{11,9},{12,... | collective-permute-start | bytes 2359304 | tf_op jit(solution)/shard_map/ppermute | solution.py:19
  21.7 1.9 collective-permute-start
  25.0 37.8 %all-gather.10.cloned.1.call-done = bf16[1,3,768,384]{3,2,1,0:T(8,128)(2,1)} async-done(((bf16[1,3,48,384]{3,2,1,0:T(8,128)(2,1)}), bf16[1,3,768,384]{3,2,1,0:T(8,128)(2,1)}) %all-gather.10.cloned.1.call-update) | async-done | bytes 1769488 | tf_op jit(solution)/shard_map/all_gather | solution.py:103
  62.7 1.8 fusion.70
  65.1 2.7 fusion.44
  67.8 40.6 %all-gather.8.cloned.1.call-done = bf16[384,2,768]{2,0,1:T(8,128)(2,1)} async-done(((bf16[24,2,768]{2,0,1:T(8,128)(2,1)}), bf16[384,2,768]{2,0,1:T(8,128)(2,1)}) %all-gather.8.cloned.1.call-update) | async-done | bytes 1179664 | tf_op jit(solution)/shard_map/all_gather | solution.py:88
  108.3 2.0 fusion.4
  110.3 1.5 fusion.102
  111.8 1.3 collective-permute-start.3
  113.1 6.9 %collective-permute-start.2 = (bf16[1,512,768]{2,1,0:T(8,128)(2,1)}, bf16[1,512,768]{2,1,0:T(8,128)(2,1)}, u32[]{:S(2)}, u32[]{:S(2)}) collective-permute-start(bf16[1,512,768]{2,1,0:T(8,128)(2,1)} %fusion.102), channel_id=1, source_target_pairs={{0,4},{1,5},{2,6},{3,7},{4,8},{5,9},{6,10},{7,11},{8,12},{9,13},{1... | collective-permute-start | bytes 2359304 | tf_op jit(solution)/shard_map/ppermute | solution.py:19
  120.8 41.3 %all-gather.12.cloned.1.call-done = bf16[1,3,768,384]{3,2,1,0:T(8,128)(2,1)} async-done(((bf16[1,3,48,384]{3,2,1,0:T(8,128)(2,1)}), bf16[1,3,768,384]{3,2,1,0:T(8,128)(2,1)}) %all-gather.12.cloned.1.call-update) | async-done | bytes 1769488 | tf_op jit(solution)/shard_map/all_gather | solution.py:103
  162.1 2.0 fusion.88
  164.1 1.7 fusion.65
  165.8 1.9 fusion.41
  167.7 0.9 fusion.60
  168.7 1.3 collective-permute-start.4
  169.9 6.1 %collective-permute-start.5 = (bf16[1,512,384]{2,1,0:T(8,128)(2,1)S(1)}, bf16[1,512,384]{2,1,0:T(8,128)(2,1)S(1)}, u32[]{:S(2)}, u32[]{:S(2)}) collective-permute-start(bf16[1,512,384]{2,1,0:T(8,128)(2,1)S(1)} %bitcast.139), channel_id=1, source_target_pairs={{0,4},{1,5},{2,6},{3,7},{4,8},{5,9},{6,10},{7,11},{8,12},{9,13},{1... | collective-permute-start | bytes 1179656 | tf_op jit(solution)/shard_map/ppermute | solution.py:19
  177.4 6.6 %collective-permute-done.4 = bf16[1,512,384]{2,1,0:T(8,128)(2,1)S(1)} collective-permute-done((bf16[1,512,384]{2,1,0:T(8,128)(2,1)S(1)}, bf16[1,512,384]{2,1,0:T(8,128)(2,1)S(1)}, u32[]{:S(2)}, u32[]{:S(2)}) %collective-permute-start.4) | collective-permute-done | bytes 393248 | tf_op jit(solution)/shard_map/ppermute | solution.py:19
  184.6 1.6 fusion.22
  187.2 1.6 pad_maximum_fusion
  188.8 74.1 %reduce-scatter.2.cloned.1.call-done = f32[24,2,768]{2,0,1:T(8,128)} async-done(((f32[384,2,768]{2,0,1:T(8,128)}), f32[24,2,768]{2,0,1:T(8,128)}) %reduce-scatter.2.cloned.1.call-update) | async-done | bytes 147472 | tf_op jit(solution)/shard_map/reduce_scatter | solution.py:146
  263.0 2.2 fusion.52
  265.2 6.5 %collective-permute-start.6 = (bf16[1,512,384]{2,1,0:T(8,128)(2,1)S(1)}, bf16[1,512,384]{2,1,0:T(8,128)(2,1)S(1)}, u32[]{:S(2)}, u32[]{:S(2)}) collective-permute-start(bf16[1,512,384]{2,1,0:T(8,128)(2,1)S(1)} %bitcast.140), channel_id=1, source_target_pairs={{2,0},{3,1},{4,2},{5,3},{6,4},{7,5},{8,6},{9,7},{10,8},{11,9},{12,... | collective-permute-start | bytes 1179656 | tf_op jit(solution)/shard_map/ppermute | solution.py:19
  271.7 2.1 collective-permute-start.7
  274.4 3.0 collective-permute-done.6
  278.1 3.5 collective-permute-done.7
  281.6 2.5 fusion.77
  284.1 152.5 %all-gather.14.cloned.1.call-done = f32[768,2,768]{2,0,1:T(8,128)} async-done(((f32[24,2,768]{2,0,1:T(8,128)}), f32[768,2,768]{2,0,1:T(8,128)}) %all-gather.14.cloned.1.call-update) | async-done | bytes 4718608 | tf_op jit(solution)/shard_map/all_gather | solution.py:12
  436.6 2.6 reduce_sum.9
  (51 shorter events, 7.8 us)
Async XLA Ops:
  7.2 16.5 %copy-start.7 = (s32[1,2]{1,0:T(1,128)S(1)}, s32[1,2]{1,0:T(1,128)}, u32[]{:S(2)}) copy-start(s32[1,2]{1,0:T(1,128)} %param.11) | copy-start | bytes 28
  7.2 17.7 %copy-start.6 = (f32[2,384]{1,0:T(2,128)S(1)}, f32[2,384]{1,0:T(2,128)}, u32[]{:S(2)}) copy-start(f32[2,384]{1,0:T(2,128)} %param.14) | copy-start | bytes 9220
  7.2 17.7 %copy-start.5 = (f32[2,384]{1,0:T(2,128)S(1)}, f32[2,384]{1,0:T(2,128)}, u32[]{:S(2)}) copy-start(f32[2,384]{1,0:T(2,128)} %param.15) | copy-start | bytes 9220
  7.2 55.5 %all-gather.10.cloned.1.call-start = ((), (), s32[]{:S(2)}) async-start(), calls=%async_computation.3 | async-start | bytes 1880064 | tf_op jit(solution)/shard_map/all_gather | solution.py:103
  8.9 99.4 %all-gather.8.cloned.1.call-start = ((), (), s32[]{:S(2)}) async-start(), calls=%async_computation.1 | async-start | bytes 1253376 | tf_op jit(solution)/shard_map/all_gather | solution.py:88
  10.5 151.5 %all-gather.12.cloned.1.call-start = ((), (), s32[]{:S(2)}) async-start(), calls=%async_computation.4 | async-start | bytes 1880064 | tf_op jit(solution)/shard_map/all_gather | solution.py:103
  11.3 251.7 %reduce-scatter.2.cloned.1.call-start = ((), (), s32[]{:S(2)}) async-start(), calls=%async_computation.2 | async-start | bytes 2506752 | tf_op jit(solution)/shard_map/reduce_scatter | solution.py:146
  13.9 50.6 %collective-permute-start.1 = (bf16[1,512,768]{2,1,0:T(8,128)(2,1)S(1)}, bf16[1,512,768]{2,1,0:T(8,128)(2,1)S(1)}, u32[]{:S(2)}, u32[]{:S(2)}) collective-permute-start(bf16[1,512,768]{2,1,0:T(8,128)(2,1)S(1)} %fusion.15), channel_id=1, source_target_pairs={{2,0},{3,1},{4,2},{5,3},{6,4},{7,5},{8,6},{9,7},{10,8},{11,9},{12,... | collective-permute-start | bytes 2359304 | tf_op jit(solution)/shard_map/ppermute | solution.py:19
  21.7 43.3 %collective-permute-start = (bf16[1,512,768]{2,1,0:T(8,128)(2,1)S(1)}, bf16[1,512,768]{2,1,0:T(8,128)(2,1)}, u32[]{:S(2)}, u32[]{:S(2)}) collective-permute-start(bf16[1,512,768]{2,1,0:T(8,128)(2,1)S(1)} %fusion.15), channel_id=1, source_target_pairs={{0,2},{1,3},{2,4},{3,5},{4,6},{5,7},{6,8},{7,9},{8,10},{9,11},{10,... | collective-permute-start | bytes 2359304 | tf_op jit(solution)/shard_map/ppermute | solution.py:19
  62.7 1.8 copy-start
  65.1 43.3 %copy-start.2 = (bf16[1,512,768]{2,1,0:T(8,128)(2,1)S(1)}, bf16[1,512,768]{2,1,0:T(8,128)(2,1)}, u32[]{:S(2)}) copy-start(bf16[1,512,768]{2,1,0:T(8,128)(2,1)} %param.9) | copy-start | bytes 2359300
  111.8 52.2 %collective-permute-start.3 = (bf16[1,512,768]{2,1,0:T(8,128)(2,1)}, bf16[1,512,768]{2,1,0:T(8,128)(2,1)}, u32[]{:S(2)}, u32[]{:S(2)}) collective-permute-start(bf16[1,512,768]{2,1,0:T(8,128)(2,1)} %fusion.102), channel_id=1, source_target_pairs={{4,0},{5,1},{6,2},{7,3},{8,4},{9,5},{10,6},{11,7},{12,8},{13,9},{1... | collective-permute-start | bytes 2359304 | tf_op jit(solution)/shard_map/ppermute | solution.py:19
  113.1 52.7 %collective-permute-start.2 = (bf16[1,512,768]{2,1,0:T(8,128)(2,1)}, bf16[1,512,768]{2,1,0:T(8,128)(2,1)}, u32[]{:S(2)}, u32[]{:S(2)}) collective-permute-start(bf16[1,512,768]{2,1,0:T(8,128)(2,1)} %fusion.102), channel_id=1, source_target_pairs={{0,4},{1,5},{2,6},{3,7},{4,8},{5,9},{6,10},{7,11},{8,12},{9,13},{1... | collective-permute-start | bytes 2359304 | tf_op jit(solution)/shard_map/ppermute | solution.py:19
  162.1 2.0 copy-start.1
  165.8 1.9 copy-start.8
  165.8 1.9 copy-start.9
  168.7 15.3 %collective-permute-start.4 = (bf16[1,512,384]{2,1,0:T(8,128)(2,1)S(1)}, bf16[1,512,384]{2,1,0:T(8,128)(2,1)S(1)}, u32[]{:S(2)}, u32[]{:S(2)}) collective-permute-start(bf16[1,512,384]{2,1,0:T(8,128)(2,1)S(1)} %bitcast.138), channel_id=1, source_target_pairs={{4,0},{5,1},{6,2},{7,3},{8,4},{9,5},{10,6},{11,7},{12,8},{13,9},{1... | collective-permute-start | bytes 1179656 | tf_op jit(solution)/shard_map/ppermute | solution.py:19
  169.9 14.7 %collective-permute-start.5 = (bf16[1,512,384]{2,1,0:T(8,128)(2,1)S(1)}, bf16[1,512,384]{2,1,0:T(8,128)(2,1)S(1)}, u32[]{:S(2)}, u32[]{:S(2)}) collective-permute-start(bf16[1,512,384]{2,1,0:T(8,128)(2,1)S(1)} %bitcast.139), channel_id=1, source_target_pairs={{0,4},{1,5},{2,6},{3,7},{4,8},{5,9},{6,10},{7,11},{8,12},{9,13},{1... | collective-permute-start | bytes 1179656 | tf_op jit(solution)/shard_map/ppermute | solution.py:19
  184.6 1.7 copy-start.3
  186.3 0.9 copy-start.10
  188.7 74.2 %copy-start.4 = (f32[512,384]{1,0:T(8,128)S(1)}, f32[512,384]{1,0:T(8,128)}, u32[]{:S(2)}) copy-start(f32[512,384]{1,0:T(8,128)} %fusion.44) | copy-start | bytes 2359300
  188.8 247.9 %all-gather.14.cloned.1.call-start = ((), (), s32[]{:S(2)}) async-start(), calls=%async_computation.5 | async-start | bytes 4866048 | tf_op jit(solution)/shard_map/all_gather | solution.py:12
  265.2 12.2 %collective-permute-start.6 = (bf16[1,512,384]{2,1,0:T(8,128)(2,1)S(1)}, bf16[1,512,384]{2,1,0:T(8,128)(2,1)S(1)}, u32[]{:S(2)}, u32[]{:S(2)}) collective-permute-start(bf16[1,512,384]{2,1,0:T(8,128)(2,1)S(1)} %bitcast.140), channel_id=1, source_target_pairs={{2,0},{3,1},{4,2},{5,3},{6,4},{7,5},{8,6},{9,7},{10,8},{11,9},{12,... | collective-permute-start | bytes 1179656 | tf_op jit(solution)/shard_map/ppermute | solution.py:19
  271.7 9.8 %collective-permute-start.7 = (bf16[1,512,384]{2,1,0:T(8,128)(2,1)S(1)}, bf16[1,512,384]{2,1,0:T(8,128)(2,1)S(1)}, u32[]{:S(2)}, u32[]{:S(2)}) collective-permute-start(bf16[1,512,384]{2,1,0:T(8,128)(2,1)S(1)} %bitcast.141), channel_id=1, source_target_pairs={{0,2},{1,3},{2,4},{3,5},{4,6},{5,7},{6,8},{7,9},{8,10},{9,11},{10,... | collective-permute-start | bytes 1179656 | tf_op jit(solution)/shard_map/ppermute | solution.py:19
  274.4 7.1 %copy-start.11 = (bf16[512,768]{1,0:T(8,128)(2,1)S(1)}, bf16[512,768]{1,0:T(8,128)(2,1)}, u32[]{:S(2)}) copy-start(bf16[512,768]{1,0:T(8,128)(2,1)} %copy-done.10) | copy-start | bytes 2359300
Sparse Core Ops, SparseCore 0:
  10.7 51.9 all-gather.9
  64.8 43.4 all-gather.7
  111.0 51.0 all-gather.11
  188.9 74.0 reduce-scatter.1
  265.9 170.6 all-gather.13
